TPU v7x, 32 devices: a whole 2x2x4 slice. The times are simulated.
32 devices in a mesh: win: 8 (over y, x, core), seq: 4 (over z).
Axes of the slice: x: 2, y: 2, z: 4, core: 2. Of those that a mesh axis runs over, the one named last changes fastest.
Arguments:
- qkv_grid: bfloat16 [90, 8, 32, 4608], P(None, 'win', 'seq'), may hold values from -160 to 160
- tokens: bfloat16 [90, 8, 32, 1536], P(None, 'win', 'seq'), may hold values from -6 to 6
- out_weight: bfloat16 [1536, 1536], replicated, may hold values from -0.625 to 0.625
- regions: int32 [90, 8, 32], P(None, 'win'), may hold values from 0 to 2, as said below
Outputs:
- mixed: bfloat16 [90, 8, 32, 1536], P(None, 'win', 'seq')
Inputs may be any that keep to these rules, and one draw needn't show every extreme that they name: `regions`: columns 2m and 2m+1 of a window always have the same region id.
All inputs are finite; a program needn't handle non-finite values.
Results may differ from a plain program's by a relative error of at most 0.01.
Values may be sent and summed in bfloat16 or wider, within the bound.
A program may use at most 128 MiB of HBM per device.

v0:
```python
import jax
import jax.numpy as jnp
from jax import lax
from jax.sharding import PartitionSpec as P

D = 1536
HEADS = 16
HD = 96
WH = 30
WW = 32


def from_behind(block, axis, distance):
    devices = range(lax.axis_size(axis))
    route = [((i - distance) % len(devices), i) for i in devices]
    return lax.ppermute(block, axis, route)


def attend(window_block, labels):
    queries = window_block[:, 0]
    key_rows = window_block[:, 1]
    values = window_block[:, 2]
    scores = jnp.einsum(
        "qhd,khd->hqk", queries, key_rows, preferred_element_type=jnp.float32
    ) * HD ** (-0.5)
    allowed = labels[:, None] == labels[None, :]
    scores = jnp.where(allowed[None], scores, -1e30)
    largest = jnp.max(scores, axis=-1, keepdims=True)
    weights = jnp.exp(scores - largest)
    soft_weights = (weights / jnp.sum(weights, axis=-1, keepdims=True)).astype(jnp.bfloat16)
    result = jnp.einsum("hqk,khd->qhd", soft_weights, values, preferred_element_type=jnp.float32)
    return result.astype(jnp.bfloat16)


def one_window(paired):
    return attend(paired[0], paired[1])


def window_attention(flat_grid, labels_flat):
    row_total, col_total, three, heads_here, head_size = flat_grid.shape
    bands = row_total // WH
    window_count = col_total // WW
    blocks = flat_grid.reshape(bands, WH, window_count, WW, three, heads_here, head_size)
    blocks = blocks.transpose(0, 2, 1, 3, 4, 5, 6).reshape(
        bands * window_count, WH * WW, three, heads_here, head_size
    )
    labels = (
        labels_flat.reshape(bands, WH, window_count, WW)
        .transpose(0, 2, 1, 3)
        .reshape(bands * window_count, WH * WW)
    )
    attended = lax.map(one_window, (blocks, labels))
    attended = attended.reshape(bands, window_count, WH, WW, heads_here, head_size).transpose(
        0, 2, 1, 3, 4, 5
    )
    return attended.reshape(row_total, col_total, heads_here, head_size)


def per_device(qkv_grid, tokens, out_weight, regions):
    seq_count = lax.axis_size("seq")
    lat_rows, win_count, col_count, packed_width = qkv_grid.shape
    labels_local = regions.reshape(lat_rows, win_count * WW)
    half_cols = WW // 2
    half_rows = WH // 2
    group_heads = HEADS // seq_count
    split_heads = qkv_grid.reshape(lat_rows, win_count, col_count, 3, seq_count, group_heads, HD)
    gathered = lax.all_to_all(split_heads, "seq", split_axis=4, concat_axis=2, tiled=True)
    flat_grid = gathered.reshape(lat_rows, win_count * WW, 3, group_heads, HD)
    arriving = from_behind(flat_grid[:, :half_cols], "win", -1)
    shifted = jnp.concatenate([flat_grid[:, half_cols:], arriving], axis=1)
    shifted = jnp.roll(shifted, -half_rows, axis=0)
    result = window_attention(shifted, labels_local)
    result = jnp.roll(result, half_rows, axis=0)
    leaving = from_behind(result[:, -half_cols:], "win", 1)
    result = jnp.concatenate([leaving, result[:, :-half_cols]], axis=1)
    attended = result.reshape(lat_rows, win_count, WW, 1, group_heads, HD)
    returned = lax.all_to_all(attended, "seq", split_axis=2, concat_axis=3, tiled=True)
    mixed_in = returned.reshape(lat_rows, win_count, col_count, D)
    projected = jnp.dot(mixed_in.reshape(-1, D), out_weight, preferred_element_type=jnp.float32)
    total = projected + tokens.reshape(-1, D).astype(jnp.float32)
    return total.astype(jnp.bfloat16).reshape(tokens.shape)


def solution(mesh):
    in_specs = (P(None, "win", "seq", None), P(None, "win", "seq", None), P(), P(None, "win", None))
    out_specs = P(None, "win", "seq", None)
    return jax.shard_map(
        per_device, mesh=mesh, in_specs=in_specs, out_specs=out_specs, check_vma=False
    )
```

profile of v0, /device:TPU:0, one launch (start us, length us, event | category | flops | bytes accessed | tf_op | source)
XLA Modules:
  0.0 490.2 jit_solution(6502701629563649295)
XLA Ops:
  0.0 17.0 %reshape.50 = bf16[90,1,8,3,4,4,96]{6,5,4,3,2,0,1:T(4,128)(2,1)} reshape(bf16[90,1,8,4608]{3,2,1,0:T(8,128)(2,1)} %param.6) | data formatting | bytes 13271040 | tf_op jit(solution)/shard_map/reshape | solution.py:66
  17.0 5.5 %copy.34 = bf16[90,1,8,3,4,4,96]{6,5,3,2,0,1,4:T(4,128)(2,1)S(1)} copy(bf16[90,1,8,3,4,4,96]{6,5,4,3,2,0,1:T(4,128)(2,1)} %reshape.50) | data formatting | bytes 13271040 | tf_op jit(solution)/shard_map/reshape | solution.py:66
  22.6 199.1 %all_to_all.30 = bf16[90,1,8,3,4,4,96]{6,5,3,2,0,1,4:T(4,128)(2,1)} all-to-all(bf16[90,1,8,3,4,4,96]{6,5,3,2,0,1,4:T(4,128)(2,1)S(1)} %copy.34), channel_id=1, replica_groups=mesh['win'=8,'seq'=4] {'seq'}, dimensions={4} | all-to-all | bytes 13271040 | tf_op jit(solution)/shard_map/all_to_all | solution.py:67
  221.7 9.7 %copy.46 = bf16[90,1,8,3,4,4,96]{6,2,4,5,3,0,1:T(8,128)(2,1)} copy(bf16[90,1,8,3,4,4,96]{6,5,3,2,0,1,4:T(4,128)(2,1)} %all_to_all.30) | data formatting | bytes 13271040 | tf_op jit(solution)/shard_map/all_to_all | solution.py:67
  231.4 0.0 copy-start.1
  231.4 9.3 %fusion.22 = (bf16[90,16,3,4,96]{4,1,3,2,0:T(8,128)(2,1)}, bf16[90,16,3,4,96]{4,1,3,2,0:T(8,128)(2,1)}) fusion(bf16[90,32,3,4,96]{4,1,3,2,0:T(8,128)(2,1)} %bitcast.76), kind=kLoop, calls=%fused_computation.39 | loop fusion | bytes 13271040 | tf_op jit(solution)/shard_map/slice | solution.py:70
  240.7 1.1 collective-permute-start
  241.8 0.0 copy-done.1
  241.8 0.1 copy.37
  241.9 0.1 reshape_transpose_reshape_reshape.3
  242.0 48.6 %collective-permute-done = bf16[90,16,3,4,96]{4,1,3,2,0:T(8,128)(2,1)} collective-permute-done((bf16[90,16,3,4,96]{4,1,3,2,0:T(8,128)(2,1)}, bf16[90,16,3,4,96]{4,1,3,2,0:T(8,128)(2,1)}, u32[]{:S(2)}, u32[]{:S(2)}) %collective-permute-start) | collective-permute-done | bytes 3317792 | tf_op jit(solution)/shard_map/ppermute | solution.py:16
  290.6 0.0 copy-start
  290.6 5.2 %fusion.15 = bf16[75,32,3,4,96]{4,1,3,2,0:T(8,128)(2,1)S(1)} fusion(bf16[90,16,3,4,96]{4,1,3,2,0:T(8,128)(2,1)} %get-tuple-element.54, bf16[90,16,3,4,96]{4,1,3,2,0:T(8,128)(2,1)} %collective-permute-done), kind=kLoop, calls=%fused_computation.27 | loop fusion | flops 11059200 | bytes 12165120 | tf_op jit(solution)/shard_map/concatenate | solution.py:70
  295.8 0.0 copy-done
  295.8 6.0 %fusion.14 = bf16[90,32,3,4,96]{4,1,3,2,0:T(8,128)(2,1)} fusion(bf16[90,16,3,4,96]{4,1,3,2,0:T(8,128)(2,1)} %collective-permute-done, bf16[90,16,3,4,96]{4,1,3,2,0:T(8,128)(2,1)S(1)} %copy-done, bf16[75,32,3,4,96]{4,1,3,2,0:T(8,128)(2,1)S(1)} %fusion.15), kind=kLoop, calls=%fused_computation.23 | loop fusion | flops 19906560 | bytes 18800640 | tf_op jit(solution)/shard_map/jit(_roll_static)/concatenate | solution.py:71
  301.8 9.0 %copy.36 = bf16[90,32,3,4,96]{4,1,0,3,2:T(8,128)(2,1)} copy(bf16[90,32,3,4,96]{4,1,3,2,0:T(8,128)(2,1)} %fusion.14) | data formatting | bytes 13271040 | tf_op jit(solution)/shard_map/jit(_roll_static)/concatenate | solution.py:71
  310.7 11.3 %copy.38 = bf16[3,960,3,4,96]{1,4,3,2,0:T(8,128)(2,1)} copy(bf16[3,960,3,4,96]{4,1,0,3,2:T(8,128)(2,1)} %bitcast.77) | data formatting | bytes 13271040 | tf_op jit(solution)/shard_map/while | solution.py:52
  322.0 59.7 %while.10 = (s32[]{:T(128)}, bf16[3,960,4,96]{1,3,2,0:T(8,128)(2,1)}, bf16[3,960,3,4,96]{1,4,3,2,0:T(8,128)(2,1)}, s32[3,960]{1,0:T(4,128)S(1)}, s32[]{:T(128)}) while((s32[]{:T(128)}, bf16[3,960,4,96]{1,3,2,0:T(8,128)(2,1)}, bf16[3,960,3,4,96]{1,4,3,2,0:T(8,128)(2,1)}, s32[3,960]{1,0:T(4,128)S(1)}, s32[]{:T(128)}) %tuple.26), condition=%wide.region_3.4_spmd, body=%wide.region_0.3_spmd.sunk | while | flops 1438987264 | bytes 39992132 | solution.py:52
  322.0 2.0 dynamic-slice_bitcast_fusion.2
  324.0 0.6 broadcast_compare_fusion.2
  324.6 9.5 %fusion.27 = (f32[4,960]{1,0:T(4,128)S(1)}, f32[4,960,960]{1,2,0:T(8,128)}) fusion(pred[960,960]{0,1:T(8,128)(4,1)S(1)} %broadcast_compare_fusion.2, bf16[960,3,4,96]{0,3,2,1:T(8,128)(2,1)S(1)} %dynamic-slice_bitcast_fusion.2), kind=kOutput, calls=%fused_computation.38.clone.1 | convolution fusion | flops 722535360 | bytes 17316864 | tf_op jit(solution)/shard_map/while/body/eval_jaxpr/sub | solution.py:29
  334.1 7.7 %fusion.28 = bf16[3,960,4,96]{1,3,2,0:T(8,128)(2,1)} fusion(bf16[3,960,4,96]{1,3,2,0:T(8,128)(2,1)} %get-tuple-element.91, s32[]{:T(128)} %get-tuple-element.90, f32[4,960,960]{1,2,0:T(8,128)} %get-tuple-element.83, f32[4,960]{1,0:T(4,128)S(1)} %get-tuple-element.84, bf16[960,3,4,96]{0,3,2,1:T(8,128)(2,1)S(1)} %dynamic-slice_bitcast_fusion.2), kind=kOutput, calls=%fused_computation.14.clone.1 | convolution fusion | flops 715530240 | bytes 17318400 | tf_op jit(solution)/shard_map/while/body/eval_jaxpr/hqk,khd->qhd/dot_general | solution.py:31
  341.9 2.0 dynamic-slice_bitcast_fusion.2
  343.9 0.6 broadcast_compare_fusion.2
  344.5 9.5 %fusion.27 = (f32[4,960]{1,0:T(4,128)S(1)}, f32[4,960,960]{1,2,0:T(8,128)}) fusion(pred[960,960]{0,1:T(8,128)(4,1)S(1)} %broadcast_compare_fusion.2, bf16[960,3,4,96]{0,3,2,1:T(8,128)(2,1)S(1)} %dynamic-slice_bitcast_fusion.2), kind=kOutput, calls=%fused_computation.38.clone.1 | convolution fusion | flops 722535360 | bytes 17316864 | tf_op jit(solution)/shard_map/while/body/eval_jaxpr/sub | solution.py:29
  354.0 7.8 %fusion.28 = bf16[3,960,4,96]{1,3,2,0:T(8,128)(2,1)} fusion(bf16[3,960,4,96]{1,3,2,0:T(8,128)(2,1)} %get-tuple-element.91, s32[]{:T(128)} %get-tuple-element.90, f32[4,960,960]{1,2,0:T(8,128)} %get-tuple-element.83, f32[4,960]{1,0:T(4,128)S(1)} %get-tuple-element.84, bf16[960,3,4,96]{0,3,2,1:T(8,128)(2,1)S(1)} %dynamic-slice_bitcast_fusion.2), kind=kOutput, calls=%fused_computation.14.clone.1 | convolution fusion | flops 715530240 | bytes 17318400 | tf_op jit(solution)/shard_map/while/body/eval_jaxpr/hqk,khd->qhd/dot_general | solution.py:31
  361.8 2.0 dynamic-slice_bitcast_fusion.2
  363.8 0.6 broadcast_compare_fusion.2
  364.4 9.5 %fusion.27 = (f32[4,960]{1,0:T(4,128)S(1)}, f32[4,960,960]{1,2,0:T(8,128)}) fusion(pred[960,960]{0,1:T(8,128)(4,1)S(1)} %broadcast_compare_fusion.2, bf16[960,3,4,96]{0,3,2,1:T(8,128)(2,1)S(1)} %dynamic-slice_bitcast_fusion.2), kind=kOutput, calls=%fused_computation.38.clone.1 | convolution fusion | flops 722535360 | bytes 17316864 | tf_op jit(solution)/shard_map/while/body/eval_jaxpr/sub | solution.py:29
  373.9 7.8 %fusion.28 = bf16[3,960,4,96]{1,3,2,0:T(8,128)(2,1)} fusion(bf16[3,960,4,96]{1,3,2,0:T(8,128)(2,1)} %get-tuple-element.91, s32[]{:T(128)} %get-tuple-element.90, f32[4,960,960]{1,2,0:T(8,128)} %get-tuple-element.83, f32[4,960]{1,0:T(4,128)S(1)} %get-tuple-element.84, bf16[960,3,4,96]{0,3,2,1:T(8,128)(2,1)S(1)} %dynamic-slice_bitcast_fusion.2), kind=kOutput, calls=%fused_computation.14.clone.1 | convolution fusion | flops 715530240 | bytes 17318400 | tf_op jit(solution)/shard_map/while/body/eval_jaxpr/hqk,khd->qhd/dot_general | solution.py:31
  381.7 3.3 copy.39
  385.0 0.4 slice.53
  385.5 0.3 fusion.20
  385.8 0.9 collective-permute-start.1
  386.7 19.2 %collective-permute-done.1 = bf16[90,16,4,96]{3,1,0,2:T(8,128)(2,1)S(1)} collective-permute-done((bf16[90,16,4,96]{3,1,0,2:T(8,128)(2,1)S(1)}, bf16[90,16,4,96]{3,1,0,2:T(8,128)(2,1)S(1)}, u32[]{:S(2)}, u32[]{:S(2)}) %collective-permute-start.1) | collective-permute-done | bytes 1105952 | tf_op jit(solution)/shard_map/ppermute | solution.py:16
  405.9 0.6 fusion.18
  406.5 2.3 copy.40
  408.7 66.9 %all_to_all.31 = bf16[90,1,32,1,4,96]{5,4,3,1,0,2:T(4,128)(2,1)S(1)} all-to-all(bf16[90,1,32,1,4,96]{5,4,3,1,0,2:T(4,128)(2,1)S(1)} %copy.40), channel_id=1, replica_groups=mesh['win'=8,'seq'=4] {'seq'}, dimensions={2} | all-to-all | bytes 4423680 | tf_op jit(solution)/shard_map/all_to_all | solution.py:77
  475.6 1.6 copy.47
  477.2 4.3 reshape_reshape.3
  481.6 8.6 %fusion.19 = bf16[90,1,8,1536]{3,2,1,0:T(8,128)(2,1)} fusion(bf16[720,1536]{1,0:T(8,128)(2,1)} %reshape_reshape.3, bf16[1536,1536]{1,0:T(8,128)(2,1)} %param.8, bf16[90,1,8,1536]{3,2,1,0:T(8,128)(2,1)} %param.7), kind=kOutput, calls=%fused_computation.36 | convolution fusion | flops 3400704000 | bytes 11354112 | tf_op jit(solution)/shard_map/dot_general | solution.py:79
  (5 shorter events, 0.1 us)
Async XLA Ops:
  231.4 10.4 %copy-start.1 = (s32[90,1,32]{0,2,1:T(8,128)S(1)}, s32[90,1,32]{0,2,1:T(8,128)}, u32[]{:S(2)}) copy-start(s32[90,1,32]{0,2,1:T(8,128)} %param.9) | copy-start | bytes 34564
  240.7 49.9 %collective-permute-start = (bf16[90,16,3,4,96]{4,1,3,2,0:T(8,128)(2,1)}, bf16[90,16,3,4,96]{4,1,3,2,0:T(8,128)(2,1)}, u32[]{:S(2)}, u32[]{:S(2)}) collective-permute-start(bf16[90,16,3,4,96]{4,1,3,2,0:T(8,128)(2,1)} %get-tuple-element.55), channel_id=1, source_target_pairs={{4,0},{8,4},{12,8},{16,12},{20,16},{24,20},{28,24},{0,28},{5,1},{9... | collective-permute-start | bytes 9953288 | tf_op jit(solution)/shard_map/ppermute | solution.py:16
  290.6 5.2 %copy-start = (bf16[90,16,3,4,96]{4,1,3,2,0:T(8,128)(2,1)S(1)}, bf16[90,16,3,4,96]{4,1,3,2,0:T(8,128)(2,1)}, u32[]{:S(2)}) copy-start(bf16[90,16,3,4,96]{4,1,3,2,0:T(8,128)(2,1)} %get-tuple-element.54) | copy-start | bytes 9953284
  385.8 20.1 %collective-permute-start.1 = (bf16[90,16,4,96]{3,1,0,2:T(8,128)(2,1)S(1)}, bf16[90,16,4,96]{3,1,0,2:T(8,128)(2,1)S(1)}, u32[]{:S(2)}, u32[]{:S(2)}) collective-permute-start(bf16[90,16,4,96]{3,1,0,2:T(8,128)(2,1)S(1)} %fusion.20), channel_id=1, source_target_pairs={{28,0},{0,4},{4,8},{8,12},{12,16},{16,20},{20,24},{24,28},{29,1},{... | collective-permute-start | bytes 3317768 | tf_op jit(solution)/shard_map/ppermute | solution.py:16
where the time goes:
time: 491 us; the launch traced here: 490 us
  blocking collectives  266 us (54%)
  local copies, waits for them, and re-layouts  80.1 us (16%)
  waiting for transfers between devices  67.8 us (14%)
  matrix products  60.3 us (12%)
  other arithmetic  13.8 us (3%)
    all_to_all x1, blocking collectives, per_device(): lax.all_to_all(split_heads, 'seq', split_axis=4, concat_axis=2, tiled=True)  199 us
    ppermute x2, waiting for transfers between devices, from_behind(): return lax.ppermute(block, axis, route)  67.8 us
    all_to_all x1, blocking collectives, per_device(): lax.all_to_all(attended, 'seq', split_axis=2, concat_axis=3, tiled=True)  66.9 us
    sub x3, matrix products, attend(): weights = jnp.exp(scores - largest)  28.4 us
    dot_general x3, matrix products, attend(): jnp.einsum('hqk,khd->qhd', soft_weights, values, preferred_element_type=j...  23.3 us
    reshape x2, local copies, waits for them, and re-layouts, per_device(): qkv_grid.reshape(lat_rows, win_count, col_count, 3, seq_count, group_head...  22.6 us
    while x2, local copies, waits for them, and re-layouts, window_attention(): attended = lax.map(one_window, (blocks, labels))  14.6 us
  transfers between devices with their start and end apart: 2, of which 2 were waited for; matrix products, arithmetic and copies ran while one was open for 0% of the time, Pallas kernels for 0%

commit v1 on v0

--- a/solution.py
+++ b/solution.py
@@ -64,7 +64,9 @@
     half_rows = WH // 2
     group_heads = HEADS // seq_count
     split_heads = qkv_grid.reshape(lat_rows, win_count, col_count, 3, seq_count, group_heads, HD)
-    gathered = lax.all_to_all(split_heads, "seq", split_axis=4, concat_axis=2, tiled=True)
+    pieces = jnp.split(split_heads, lax.axis_size("seq"), axis=4)
+    arrived = lax.all_to_all(jnp.stack(pieces), "seq", 0, 0)
+    gathered = jnp.concatenate(arrived, axis=2)
     flat_grid = gathered.reshape(lat_rows, win_count * WW, 3, group_heads, HD)
     arriving = from_behind(flat_grid[:, :half_cols], "win", -1)
     shifted = jnp.concatenate([flat_grid[:, half_cols:], arriving], axis=1)

time: 491 us -> 501 us (1.020)
  other arithmetic: 13.8 us -> 23.1 us
    all_to_all x1 -> x0, local copies, waits for them, and re-layouts: 9.7 us -> none  [per_device(): lax.all_to_all(split_heads, 'seq', split_axis=4, concat_axis=2, tiled=True)]
    reshape x0 -> x1, local copies, waits for them, and re-layouts: none -> 9.7 us  [per_device(): gathered = jnp.concatenate(arrived, axis=2)]
    another operation x0 -> x1, other arithmetic: none -> 9.27 us  [per_device(): arrived = lax.all_to_all(jnp.stack(pieces), 'seq', 0, 0)]
    reshape x2 -> x1, local copies, waits for them, and re-layouts: 22.6 us -> 17 us  [per_device(): qkv_grid.reshape(lat_rows, win_count, col_count, 3, seq_count, group_head...]
    another operation x0 -> x1, local copies, waits for them, and re-layouts: none -> 5.51 us  [per_device(): arrived = lax.all_to_all(jnp.stack(pieces), 'seq', 0, 0)]
where the time goes in v1:
time: 501 us; the launch traced here: 500 us
  blocking collectives  266 us (53%)
  local copies, waits for them, and re-layouts  80.1 us (16%)
  waiting for transfers between devices  67.8 us (14%)
  matrix products  60.4 us (12%)
  other arithmetic  23.1 us (5%)
    all_to_all x1, blocking collectives, per_device(): arrived = lax.all_to_all(jnp.stack(pieces), 'seq', 0, 0)  199 us
    ppermute x2, waiting for transfers between devices, from_behind(): return lax.ppermute(block, axis, route)  67.8 us
    all_to_all x1, blocking collectives, per_device(): lax.all_to_all(attended, 'seq', split_axis=2, concat_axis=3, tiled=True)  66.9 us
    sub x3, matrix products, attend(): weights = jnp.exp(scores - largest)  28.5 us
    dot_general x3, matrix products, attend(): jnp.einsum('hqk,khd->qhd', soft_weights, values, preferred_element_type=j...  23.3 us
    reshape x1, local copies, waits for them, and re-layouts, per_device(): qkv_grid.reshape(lat_rows, win_count, col_count, 3, seq_count, group_head...  17 us
    while x2, local copies, waits for them, and re-layouts, window_attention(): attended = lax.map(one_window, (blocks, labels))  14.6 us
  transfers between devices with their start and end apart: 2, of which 2 were waited for; matrix products, arithmetic and copies ran while one was open for 0% of the time, Pallas kernels for 0%

profile of v1, /device:TPU:0, one launch (start us, length us, event | category | flops | bytes accessed | tf_op | source)
XLA Modules:
  0.0 499.5 jit_solution(17035862254099834257)
XLA Ops:
  0.0 17.0 %reshape.49 = bf16[90,1,8,3,4,4,96]{6,5,4,3,2,0,1:T(4,128)(2,1)} reshape(bf16[90,1,8,4608]{3,2,1,0:T(8,128)(2,1)} %param.6) | data formatting | bytes 13271040 | tf_op jit(solution)/shard_map/reshape | solution.py:66
  17.0 5.5 %slice_bitcast_fusion.17 = (bf16[1,90,1,8,3,1,4,96]{7,6,4,3,1,5,2,0:T(4,128)(2,1)S(1)}, bf16[1,90,1,8,3,1,4,96]{7,6,4,3,1,5,2,0:T(4,128)(2,1)S(1)}, bf16[1,90,1,...) fusion(bf16[90,1,8,3,4,4,96]{6,5,4,3,2,0,1:T(4,128)(2,1)} %reshape.49), kind=kLoop, calls=%fused_computation.41 | loop fusion | bytes 13271040 | tf_op jit(solution)/shard_map/stack | solution.py:68
  22.6 9.3 %pad_maximum_fusion.1 = bf16[4,90,1,8,3,1,4,96]{7,6,4,3,1,5,2,0:T(4,128)(2,1)S(1)} fusion(bf16[1,90,1,8,3,1,4,96]{7,6,4,3,1,5,2,0:T(4,128)(2,1)S(1)} %get-tuple-element.58, bf16[1,90,1,8,3,1,4,96]{7,6,4,3,1,5,2,0:T(4,128)(2,1)S(1)} %get-tuple-element.59, bf16[1,90,1,8,3,1,4,96]{7,6,4,3,1,5,2,0:T(4,128)(2,1)S(1)} %get-tuple-element.57, ...), kind=kLoop, calls=%fused_computation.24 | loop fusion | flops 9953280 | bytes 13271040 | tf_op jit(solution)/shard_map/stack | solution.py:68
  31.8 199.1 %all_to_all.20 = bf16[4,90,1,8,3,1,4,96]{7,6,4,3,1,5,2,0:T(4,128)(2,1)} all-to-all(bf16[4,90,1,8,3,1,4,96]{7,6,4,3,1,5,2,0:T(4,128)(2,1)S(1)} %pad_maximum_fusion.1), channel_id=1, replica_groups=mesh['win'=8,'seq'=4] {'seq'}, dimensions={0} | all-to-all | bytes 13271040 | tf_op jit(solution)/shard_map/all_to_all | solution.py:68
  230.9 9.7 %copy.62 = bf16[90,1,4,8,3,1,4,96]{7,3,2,6,4,0,5,1:T(8,128)(2,1)} copy(bf16[90,1,4,8,3,1,4,96]{7,6,4,3,0,5,1,2:T(4,128)(2,1)} %bitcast.88) | data formatting | bytes 13271040 | tf_op jit(solution)/shard_map/reshape | solution.py:69
  240.6 0.0 copy-start.1
  240.6 9.3 %fusion.22 = (bf16[90,16,3,4,96]{4,1,3,2,0:T(8,128)(2,1)}, bf16[90,16,3,4,96]{4,1,3,2,0:T(8,128)(2,1)}) fusion(bf16[90,32,3,4,96]{4,1,3,2,0:T(8,128)(2,1)} %bitcast.87), kind=kLoop, calls=%fused_computation.44 | loop fusion | bytes 13271040 | tf_op jit(solution)/shard_map/slice | solution.py:72
  250.0 1.1 collective-permute-start
  251.1 0.0 copy-done.1
  251.1 0.1 copy.50
  251.2 0.1 reshape_transpose_reshape_reshape.3
  251.3 48.6 %collective-permute-done = bf16[90,16,3,4,96]{4,1,3,2,0:T(8,128)(2,1)} collective-permute-done((bf16[90,16,3,4,96]{4,1,3,2,0:T(8,128)(2,1)}, bf16[90,16,3,4,96]{4,1,3,2,0:T(8,128)(2,1)}, u32[]{:S(2)}, u32[]{:S(2)}) %collective-permute-start) | collective-permute-done | bytes 3317792 | tf_op jit(solution)/shard_map/ppermute | solution.py:16
  299.9 0.0 copy-start
  299.9 5.2 %fusion.15 = bf16[75,32,3,4,96]{4,1,3,2,0:T(8,128)(2,1)S(1)} fusion(bf16[90,16,3,4,96]{4,1,3,2,0:T(8,128)(2,1)} %get-tuple-element.54, bf16[90,16,3,4,96]{4,1,3,2,0:T(8,128)(2,1)} %collective-permute-done), kind=kLoop, calls=%fused_computation.28 | loop fusion | flops 11059200 | bytes 12165120 | tf_op jit(solution)/shard_map/concatenate | solution.py:72
  305.0 0.0 copy-done
  305.1 6.0 %fusion.14 = bf16[90,32,3,4,96]{4,1,3,2,0:T(8,128)(2,1)} fusion(bf16[90,16,3,4,96]{4,1,3,2,0:T(8,128)(2,1)} %collective-permute-done, bf16[90,16,3,4,96]{4,1,3,2,0:T(8,128)(2,1)S(1)} %copy-done, bf16[75,32,3,4,96]{4,1,3,2,0:T(8,128)(2,1)S(1)} %fusion.15), kind=kLoop, calls=%fused_computation.23 | loop fusion | flops 19906560 | bytes 18800640 | tf_op jit(solution)/shard_map/jit(_roll_static)/concatenate | solution.py:73
  311.0 9.0 %copy.49 = bf16[90,32,3,4,96]{4,1,0,3,2:T(8,128)(2,1)} copy(bf16[90,32,3,4,96]{4,1,3,2,0:T(8,128)(2,1)} %fusion.14) | data formatting | bytes 13271040 | tf_op jit(solution)/shard_map/jit(_roll_static)/concatenate | solution.py:73
  320.0 11.3 %copy.51 = bf16[3,960,3,4,96]{1,4,3,2,0:T(8,128)(2,1)} copy(bf16[3,960,3,4,96]{4,1,0,3,2:T(8,128)(2,1)} %bitcast.89) | data formatting | bytes 13271040 | tf_op jit(solution)/shard_map/while | solution.py:52
  331.3 59.8 %while.10 = (s32[]{:T(128)}, bf16[3,960,4,96]{1,3,2,0:T(8,128)(2,1)}, bf16[3,960,3,4,96]{1,4,3,2,0:T(8,128)(2,1)}, s32[3,960]{1,0:T(4,128)S(1)}, s32[]{:T(128)}) while((s32[]{:T(128)}, bf16[3,960,4,96]{1,3,2,0:T(8,128)(2,1)}, bf16[3,960,3,4,96]{1,4,3,2,0:T(8,128)(2,1)}, s32[3,960]{1,0:T(4,128)S(1)}, s32[]{:T(128)}) %tuple.29), condition=%wide.region_3.4_spmd, body=%wide.region_0.3_spmd.sunk | while | flops 1438987264 | bytes 39992132 | solution.py:52
  331.3 2.0 dynamic-slice_bitcast_fusion.2
  333.3 0.6 broadcast_compare_fusion.2
  333.9 9.5 %fusion.27 = (f32[4,960]{1,0:T(4,128)S(1)}, f32[4,960,960]{1,2,0:T(8,128)}) fusion(pred[960,960]{0,1:T(8,128)(4,1)S(1)} %broadcast_compare_fusion.2, bf16[960,3,4,96]{0,3,2,1:T(8,128)(2,1)S(1)} %dynamic-slice_bitcast_fusion.2), kind=kOutput, calls=%fused_computation.43.clone.1 | convolution fusion | flops 722535360 | bytes 17316864 | tf_op jit(solution)/shard_map/while/body/eval_jaxpr/sub | solution.py:29
  343.4 7.8 %fusion.28 = bf16[3,960,4,96]{1,3,2,0:T(8,128)(2,1)} fusion(bf16[3,960,4,96]{1,3,2,0:T(8,128)(2,1)} %get-tuple-element.95, s32[]{:T(128)} %get-tuple-element.94, f32[4,960,960]{1,2,0:T(8,128)} %get-tuple-element.87, f32[4,960]{1,0:T(4,128)S(1)} %get-tuple-element.88, bf16[960,3,4,96]{0,3,2,1:T(8,128)(2,1)S(1)} %dynamic-slice_bitcast_fusion.2), kind=kOutput, calls=%fused_computation.14.clone.1 | convolution fusion | flops 715530240 | bytes 17318400 | tf_op jit(solution)/shard_map/while/body/eval_jaxpr/hqk,khd->qhd/dot_general | solution.py:31
  351.2 2.0 dynamic-slice_bitcast_fusion.2
  353.2 0.6 broadcast_compare_fusion.2
  353.9 9.5 %fusion.27 = (f32[4,960]{1,0:T(4,128)S(1)}, f32[4,960,960]{1,2,0:T(8,128)}) fusion(pred[960,960]{0,1:T(8,128)(4,1)S(1)} %broadcast_compare_fusion.2, bf16[960,3,4,96]{0,3,2,1:T(8,128)(2,1)S(1)} %dynamic-slice_bitcast_fusion.2), kind=kOutput, calls=%fused_computation.43.clone.1 | convolution fusion | flops 722535360 | bytes 17316864 | tf_op jit(solution)/shard_map/while/body/eval_jaxpr/sub | solution.py:29
  363.3 7.8 %fusion.28 = bf16[3,960,4,96]{1,3,2,0:T(8,128)(2,1)} fusion(bf16[3,960,4,96]{1,3,2,0:T(8,128)(2,1)} %get-tuple-element.95, s32[]{:T(128)} %get-tuple-element.94, f32[4,960,960]{1,2,0:T(8,128)} %get-tuple-element.87, f32[4,960]{1,0:T(4,128)S(1)} %get-tuple-element.88, bf16[960,3,4,96]{0,3,2,1:T(8,128)(2,1)S(1)} %dynamic-slice_bitcast_fusion.2), kind=kOutput, calls=%fused_computation.14.clone.1 | convolution fusion | flops 715530240 | bytes 17318400 | tf_op jit(solution)/shard_map/while/body/eval_jaxpr/hqk,khd->qhd/dot_general | solution.py:31
  371.1 2.0 dynamic-slice_bitcast_fusion.2
  373.2 0.6 broadcast_compare_fusion.2
  373.8 9.5 %fusion.27 = (f32[4,960]{1,0:T(4,128)S(1)}, f32[4,960,960]{1,2,0:T(8,128)}) fusion(pred[960,960]{0,1:T(8,128)(4,1)S(1)} %broadcast_compare_fusion.2, bf16[960,3,4,96]{0,3,2,1:T(8,128)(2,1)S(1)} %dynamic-slice_bitcast_fusion.2), kind=kOutput, calls=%fused_computation.43.clone.1 | convolution fusion | flops 722535360 | bytes 17316864 | tf_op jit(solution)/shard_map/while/body/eval_jaxpr/sub | solution.py:29
  383.3 7.8 %fusion.28 = bf16[3,960,4,96]{1,3,2,0:T(8,128)(2,1)} fusion(bf16[3,960,4,96]{1,3,2,0:T(8,128)(2,1)} %get-tuple-element.95, s32[]{:T(128)} %get-tuple-element.94, f32[4,960,960]{1,2,0:T(8,128)} %get-tuple-element.87, f32[4,960]{1,0:T(4,128)S(1)} %get-tuple-element.88, bf16[960,3,4,96]{0,3,2,1:T(8,128)(2,1)S(1)} %dynamic-slice_bitcast_fusion.2), kind=kOutput, calls=%fused_computation.14.clone.1 | convolution fusion | flops 715530240 | bytes 17318400 | tf_op jit(solution)/shard_map/while/body/eval_jaxpr/hqk,khd->qhd/dot_general | solution.py:31
  391.0 3.3 copy.52
  394.3 0.4 slice.53
  394.8 0.3 fusion.20
  395.1 0.9 collective-permute-start.1
  396.0 19.2 %collective-permute-done.1 = bf16[90,16,4,96]{3,1,0,2:T(8,128)(2,1)S(1)} collective-permute-done((bf16[90,16,4,96]{3,1,0,2:T(8,128)(2,1)S(1)}, bf16[90,16,4,96]{3,1,0,2:T(8,128)(2,1)S(1)}, u32[]{:S(2)}, u32[]{:S(2)}) %collective-permute-start.1) | collective-permute-done | bytes 1105952 | tf_op jit(solution)/shard_map/ppermute | solution.py:16
  415.2 0.6 fusion.18
  415.8 2.3 copy.53
  418.1 66.9 %all_to_all.21 = bf16[90,1,32,1,4,96]{5,4,3,1,0,2:T(4,128)(2,1)S(1)} all-to-all(bf16[90,1,32,1,4,96]{5,4,3,1,0,2:T(4,128)(2,1)S(1)} %copy.53), channel_id=1, replica_groups=mesh['win'=8,'seq'=4] {'seq'}, dimensions={2} | all-to-all | bytes 4423680 | tf_op jit(solution)/shard_map/all_to_all | solution.py:79
  484.9 1.6 copy.63
  486.6 4.3 reshape_reshape.7
  490.9 8.6 %fusion.19 = bf16[90,1,8,1536]{3,2,1,0:T(8,128)(2,1)} fusion(bf16[720,1536]{1,0:T(8,128)(2,1)} %reshape_reshape.7, bf16[1536,1536]{1,0:T(8,128)(2,1)} %param.8, bf16[90,1,8,1536]{3,2,1,0:T(8,128)(2,1)} %param.7), kind=kOutput, calls=%fused_computation.37 | convolution fusion | flops 3400704000 | bytes 11354112 | tf_op jit(solution)/shard_map/dot_general | solution.py:81
  (5 shorter events, 0.1 us)
Async XLA Ops:
  240.6 10.4 %copy-start.1 = (s32[90,1,32]{0,2,1:T(8,128)S(1)}, s32[90,1,32]{0,2,1:T(8,128)}, u32[]{:S(2)}) copy-start(s32[90,1,32]{0,2,1:T(8,128)} %param.9) | copy-start | bytes 34564
  250.0 49.9 %collective-permute-start = (bf16[90,16,3,4,96]{4,1,3,2,0:T(8,128)(2,1)}, bf16[90,16,3,4,96]{4,1,3,2,0:T(8,128)(2,1)}, u32[]{:S(2)}, u32[]{:S(2)}) collective-permute-start(bf16[90,16,3,4,96]{4,1,3,2,0:T(8,128)(2,1)} %get-tuple-element.55), channel_id=1, source_target_pairs={{4,0},{8,4},{12,8},{16,12},{20,16},{24,20},{28,24},{0,28},{5,1},{9... | collective-permute-start | bytes 9953288 | tf_op jit(solution)/shard_map/ppermute | solution.py:16
  299.9 5.2 %copy-start = (bf16[90,16,3,4,96]{4,1,3,2,0:T(8,128)(2,1)S(1)}, bf16[90,16,3,4,96]{4,1,3,2,0:T(8,128)(2,1)}, u32[]{:S(2)}) copy-start(bf16[90,16,3,4,96]{4,1,3,2,0:T(8,128)(2,1)} %get-tuple-element.54) | copy-start | bytes 9953284
  395.1 20.1 %collective-permute-start.1 = (bf16[90,16,4,96]{3,1,0,2:T(8,128)(2,1)S(1)}, bf16[90,16,4,96]{3,1,0,2:T(8,128)(2,1)S(1)}, u32[]{:S(2)}, u32[]{:S(2)}) collective-permute-start(bf16[90,16,4,96]{3,1,0,2:T(8,128)(2,1)S(1)} %fusion.20), channel_id=1, source_target_pairs={{28,0},{0,4},{4,8},{8,12},{12,16},{16,20},{20,24},{24,28},{29,1},{... | collective-permute-start | bytes 3317768 | tf_op jit(solution)/shard_map/ppermute | solution.py:16
